TPU v7x, 256 devices: a whole 4x4x8 slice. The times are simulated.
256 devices in a mesh: grp: 2 (over core), row: 4 (over y), col: 32 (over z, x).
Axes of the slice: x: 4, y: 4, z: 8, core: 2. Of those that a mesh axis runs over, the one named last changes fastest.
Arguments:
- sub_rhs: float32 [2, 3, 4, 32, 256, 512], P('grp', None, 'row', 'col'), may hold values from -6 to 6
- sub_dinv: float32 [2, 3, 4, 32, 256, 256], P('grp', None, 'row', 'col')
- anc_rhs: float32 [4, 32, 256, 512], P('row', 'col'), may hold values from -6 to 6
- anc_dinv: float32 [4, 32, 256, 256], P('row', 'col')
- tiles: bfloat16 [2, 4, 32, 3, 16, 256, 256], P('grp', 'row', 'col'), may hold values from -0.09375 to 0.09375
- tile_target: int32 [2, 4, 32, 3, 16], P('grp', 'row', 'col'), may hold values from 0 to 11, as said below
- tile_source: int32 [2, 4, 32, 3, 16], P('grp', 'row', 'col'), may hold values from 0 to 31, as said below
- tile_count: int32 [2, 4, 32, 3], P('grp', 'row', 'col'), may hold values from 1 to 16, as said below
Outputs:
- sub_solution: float32 [2, 3, 4, 32, 256, 512], P('grp', None, 'row', 'col')
- anc_solution: float32 [4, 32, 256, 512], P('row', 'col')
Inputs may be any that keep to these rules, and one draw needn't show every extreme that they name: `tile_target`: entry [g, q, c, k, j] is (t - 1) * 4 + r for a target level t with k < t <= 3 (t = 3 is the ancestor level) and a process row r; entries at slots j >= tile_count are unused. `tile_source`: Non-decreasing along the last dimension. `tile_count`: for every source level some device holds exactly 16 live tiles.
All inputs are finite; a program needn't handle non-finite values.
Results may differ from a plain program's by a relative error of at most 0.0027.
Values may be sent and summed in bfloat16 or wider, within the bound.
No kernel may reach another device: no remote copies, remote signals or barrier semaphores. Data moves between devices by JAX's collectives and lax.ppermute only.
A program may use at most 128 MiB of HBM per device.

v0:
```python
import jax
import jax.numpy as jnp
from jax import lax
from jax.sharding import PartitionSpec as P


def split_up(shard, dim, peers):
    lengths = shard.shape
    pieces = shard.reshape(*lengths[:dim], peers, lengths[dim] // peers, *lengths[dim + 1 :])
    return jnp.moveaxis(pieces, dim, 0)


def sum_at_owner(shard, axis, dim):
    peers = lax.axis_size(axis)
    pieces = lax.all_to_all(split_up(shard, dim, peers), axis, 0, 0, tiled=True)
    return jnp.sum(pieces, axis=0)


def from_everyone(shard, axis):
    copies = jnp.broadcast_to(shard, (lax.axis_size(axis), *shard.shape))
    return lax.all_to_all(copies, axis, split_axis=0, concat_axis=0, tiled=True)


def of_everyone(shard, axis):
    return from_everyone(shard, axis).sum(axis=0)


def spread_terms(pending, gathered, blocks, targets, sources, live_count):
    slots = blocks.shape[0]
    fetched = jnp.take(gathered, sources, axis=0)
    products = jnp.einsum("tij,tjw->tiw", blocks, fetched, preferred_element_type=jnp.float32)
    live = jnp.arange(slots, dtype=jnp.int32) < live_count
    codes = jnp.arange(pending.shape[0], dtype=jnp.int32)
    selector = ((targets[:, None] == codes[None, :]) & live[:, None]).astype(jnp.float32)
    return pending + jnp.einsum("tk,tiw->kiw", selector, products, precision=lax.Precision.HIGHEST)


def on_device(sub_rhs, sub_dinv, anc_rhs, anc_dinv, tiles, tile_target, tile_source, tile_count):
    highest = lax.Precision.HIGHEST
    rhs_levels = sub_rhs[0, :, 0, 0]
    inverses = sub_dinv[0, :, 0, 0]
    blocks = tiles[0, 0, 0]
    targets = tile_target[0, 0, 0]
    sources = tile_source[0, 0, 0]
    counts = tile_count[0, 0, 0]
    depth, block_rows, columns = rhs_levels.shape
    row_count = lax.axis_size("row")
    pending = jnp.zeros((depth * row_count, block_rows, columns), jnp.float32)
    solved = []
    for source_level in range(depth):
        remainder = rhs_levels[source_level]
        if source_level > 0:
            arrived = sum_at_owner(
                pending[(source_level - 1) * row_count : source_level * row_count], "row", 0
            )
            remainder = remainder - arrived[0]
        current = jnp.dot(
            inverses[source_level], remainder, precision=highest, preferred_element_type=jnp.float32
        )
        solved.append(current)
        rounded = current.astype(jnp.bfloat16)[None]
        everyone = lax.all_gather(rounded, "col", axis=0, tiled=True)
        pending = spread_terms(
            pending,
            everyone,
            blocks[source_level],
            targets[source_level],
            sources[source_level],
            counts[source_level],
        )
    ancestor_part = pending[(depth - 1) * row_count :]
    ancestor_rhs = anc_rhs[0, 0]
    ancestor_inverse = anc_dinv[0, 0]
    group_part = sum_at_owner(ancestor_part, "row", 0)[0]
    combined = of_everyone(group_part, "grp")
    ancestor = jnp.dot(
        ancestor_inverse,
        ancestor_rhs - combined,
        precision=highest,
        preferred_element_type=jnp.float32,
    )
    sub_out = jnp.stack(solved)[None, :, None, None]
    return (sub_out, ancestor[None, None])


def solution(mesh):
    placed = (
        P("grp", None, "row", "col", None, None),
        P("grp", None, "row", "col", None, None),
        P("row", "col", None, None),
        P("row", "col", None, None),
        P("grp", "row", "col", None, None, None, None),
        P("grp", "row", "col", None, None),
        P("grp", "row", "col", None, None),
        P("grp", "row", "col", None),
    )
    return jax.shard_map(
        on_device,
        mesh=mesh,
        in_specs=placed,
        out_specs=(P("grp", None, "row", "col", None, None), P("row", "col", None, None)),
        check_vma=False,
    )
```

profile of v0, /device:TPU:1, one launch (start us, length us, event | category | flops | bytes accessed | tf_op | source)
XLA Modules:
  0.0 535.7 jit_solution(11485842534469327376)
XLA Ops:
  13.2 99.7 %all-gather.7.cloned.1.call-done = bf16[8192,512]{1,0:T(8,128)(2,1)} async-done(((bf16[256,512]{1,0:T(8,128)(2,1)}), bf16[8192,512]{1,0:T(8,128)(2,1)}) %all-gather.7.cloned.1.call-update) | async-done | bytes 8388624 | tf_op jit(solution)/shard_map/all_gather | solution.py:62
  112.9 6.2 %gather_fusion = bf16[16,256,512]{2,1,0:T(8,128)(2,1)} fusion(bf16[32,256,512]{2,1,0:T(8,128)(2,1)} %bitcast.126, s32[1024]{0:T(1024)S(1)} %pad_clamp_fusion.2), kind=kCustom, calls=%fused_computation.clone | custom fusion | bytes 8388672 | tf_op jit(solution)/shard_map/jit(_take)/gather | solution.py:30
  119.1 7.6 %fusion.9 = f32[16,256,512]{1,2,0:T(8,128)} fusion(bf16[16,256,512]{2,1,0:T(8,128)(2,1)} %gather_fusion, pred[16]{0:T(512)(128)(4,1)S(1)} %get-tuple-element.20, bf16[1,1,1,3,16,256,256]{6,5,4,3,2,1,0:T(8,128)(2,1)} %param.14), kind=kOutput, calls=%fused_computation.13 | convolution fusion | flops 1075838976 | bytes 14680080 | tf_op jit(solution)/shard_map/tij,tjw->tiw/dot_general | solution.py:31
  126.7 10.5 %copy.32 = f32[16,256,512]{2,0,1:T(8,128)} copy(f32[16,256,512]{1,2,0:T(8,128)} %fusion.9) | data formatting | bytes 16777216 | tf_op jit(solution)/shard_map/tij,tjw->tiw/dot_general | solution.py:31
  137.2 12.8 %fusion.47 = f32[12,256,512]{2,0,1:T(8,128)S(1)} fusion(f32[16,256,512]{2,0,1:T(8,128)} %copy.32, s32[16]{0:T(128)S(1)} %get-tuple-element.18, pred[16]{0:T(512)(128)(4,1)S(1)} %iota_compare_fusion.5), kind=kOutput, calls=%fused_computation.58 | convolution fusion | flops 301990272 | bytes 14680144 | tf_op jit(solution)/shard_map/tk,tiw->kiw/dot_general | solution.py:35
  149.9 3.2 copy-done.1
  154.4 28.5 %all_to_all.20 = f32[4,1,256,512]{3,2,1,0:T(8,128)S(1)} all-to-all(f32[4,1,256,512]{3,2,1,0:T(8,128)S(1)} %copy.33), channel_id=1, replica_groups=mesh['grp'=2,'row'=4,'col'=32] {'row'}, dimensions={0} | all-to-all | bytes 4194304 | tf_op jit(solution)/shard_map/all_to_all | solution.py:15
  187.4 94.4 %all-gather.9.cloned.1.call-done = bf16[8192,512]{1,0:T(8,128)(2,1)} async-done(((bf16[256,512]{1,0:T(8,128)(2,1)}), bf16[8192,512]{1,0:T(8,128)(2,1)}) %all-gather.9.cloned.1.call-update) | async-done | bytes 8388624 | tf_op jit(solution)/shard_map/all_gather | solution.py:62
  281.8 6.1 %gather_fusion.1 = bf16[16,256,512]{2,1,0:T(8,128)(2,1)} fusion(bf16[32,256,512]{2,1,0:T(8,128)(2,1)} %bitcast.127, s32[1024]{0:T(1024)S(1)} %pad_clamp_fusion.1), kind=kCustom, calls=%fused_computation.1.clone | custom fusion | bytes 8388672 | tf_op jit(solution)/shard_map/jit(_take)/gather | solution.py:30
  287.9 7.6 %fusion.12 = f32[16,256,512]{1,2,0:T(8,128)} fusion(bf16[16,256,512]{2,1,0:T(8,128)(2,1)} %gather_fusion.1, pred[16]{0:T(512)(128)(4,1)S(1)} %get-tuple-element.22, bf16[1,1,1,3,16,256,256]{6,5,4,3,2,1,0:T(8,128)(2,1)} %param.14), kind=kOutput, calls=%fused_computation.14 | convolution fusion | flops 1075838976 | bytes 14680080 | tf_op jit(solution)/shard_map/tij,tjw->tiw/dot_general | solution.py:31
  295.5 10.5 %copy.36 = f32[16,256,512]{2,0,1:T(8,128)} copy(f32[16,256,512]{1,2,0:T(8,128)} %fusion.12) | data formatting | bytes 16777216 | tf_op jit(solution)/shard_map/tij,tjw->tiw/dot_general | solution.py:31
  306.0 10.9 %convolution_add_fusion = f32[12,256,512]{2,0,1:T(8,128)S(1)} fusion(f32[12,256,512]{2,0,1:T(8,128)} %copy-done.1, f32[16,256,512]{2,0,1:T(8,128)} %copy.36, s32[16]{0:T(128)S(1)} %get-tuple-element.19, pred[16]{0:T(512)(128)(4,1)S(1)} %iota_compare_fusion.4), kind=kOutput, calls=%fused_computation.12 | convolution fusion | flops 303563136 | bytes 20971600 | tf_op jit(solution)/shard_map/tk,tiw->kiw/dot_general | solution.py:35
  316.9 3.2 copy-done.2
  321.4 28.5 %all_to_all.21 = f32[4,1,256,512]{3,2,1,0:T(8,128)S(1)} all-to-all(f32[4,1,256,512]{3,2,1,0:T(8,128)S(1)} %copy.37), channel_id=1, replica_groups=mesh['grp'=2,'row'=4,'col'=32] {'row'}, dimensions={0} | all-to-all | bytes 4194304 | tf_op jit(solution)/shard_map/all_to_all | solution.py:15
  350.9 2.8 bitcast_convert_fusion
  354.4 94.6 %all-gather.11.cloned.1.call-done = bf16[8192,512]{1,0:T(8,128)(2,1)} async-done(((bf16[256,512]{1,0:T(8,128)(2,1)}), bf16[8192,512]{1,0:T(8,128)(2,1)}) %all-gather.11.cloned.1.call-update) | async-done | bytes 8388624 | tf_op jit(solution)/shard_map/all_gather | solution.py:62
  449.0 6.1 %gather_fusion.2 = bf16[16,256,512]{2,1,0:T(8,128)(2,1)} fusion(bf16[32,256,512]{2,1,0:T(8,128)(2,1)} %bitcast.128, s32[1024]{0:T(1024)S(1)} %pad_clamp_fusion), kind=kCustom, calls=%fused_computation.2.clone | custom fusion | bytes 8388672 | tf_op jit(solution)/shard_map/jit(_take)/gather | solution.py:30
  455.1 7.6 %fusion.15 = f32[16,256,512]{1,2,0:T(8,128)} fusion(bf16[16,256,512]{2,1,0:T(8,128)(2,1)} %gather_fusion.2, pred[16]{0:T(512)(128)(4,1)S(1)} %get-tuple-element.11, bf16[1,1,1,3,16,256,256]{6,5,4,3,2,1,0:T(8,128)(2,1)} %param.14), kind=kOutput, calls=%fused_computation.15 | convolution fusion | flops 1075838976 | bytes 14680080 | tf_op jit(solution)/shard_map/tij,tjw->tiw/dot_general | solution.py:31
  462.7 10.5 %copy.40 = f32[16,256,512]{2,0,1:T(8,128)} copy(f32[16,256,512]{1,2,0:T(8,128)} %fusion.15) | data formatting | bytes 16777216 | tf_op jit(solution)/shard_map/tij,tjw->tiw/dot_general | solution.py:31
  473.2 12.8 %fusion.54 = f32[12,256,512]{2,0,1:T(8,128)S(1)} fusion(f32[16,256,512]{2,0,1:T(8,128)} %copy.40, s32[16]{0:T(128)S(1)} %get-tuple-element.17, pred[16]{0:T(512)(128)(4,1)S(1)} %iota_compare_fusion.3), kind=kOutput, calls=%fused_computation.63 | convolution fusion | flops 301990272 | bytes 14680144 | tf_op jit(solution)/shard_map/tk,tiw->kiw/dot_general | solution.py:35
  485.9 3.2 fusion.18
  491.1 4.0 all-to-all-start.2
  497.4 22.7 %all-to-all-done.2 = f32[4,1,256,512]{3,2,1,0:T(8,128)S(1)} async-done(((f32[4,1,256,512]{3,2,1,0:T(8,128)}), f32[4,1,256,512]{3,2,1,0:T(8,128)S(1)}, u32[]{:S(2)}, u32[]{:S(2)}) %all-to-all-start.2) | async-done | bytes 2097184 | tf_op jit(solution)/shard_map/all_to_all | solution.py:15
  520.5 6.5 %all_to_all.22 = f32[2,256,512]{2,1,0:T(8,128)S(1)} all-to-all(f32[2,256,512]{2,1,0:T(8,128)S(1)} %broadcast_in_dim.37), channel_id=1, replica_groups=mesh['grp'=2,'row'=4,'col'=32] {'grp'}, dimensions={0} | all-to-all | bytes 2097152 | tf_op jit(solution)/shard_map/all_to_all | solution.py:21
  (36 shorter events, 21.5 us)
Async XLA Ops:
  7.2 519.9 %copy-start = (f32[1,1,256,256]{3,2,1,0:T(8,128)S(1)}, f32[1,1,256,256]{3,2,1,0:T(8,128)}, u32[]{:S(2)}) copy-start(f32[1,1,256,256]{3,2,1,0:T(8,128)} %param.13) | copy-start | bytes 786436
  7.2 105.7 %all-gather.7.cloned.1.call-start = ((), (), s32[]{:S(2)}) async-start(), calls=%async_computation.4 | async-start | bytes 8650752 | tf_op jit(solution)/shard_map/all_gather | solution.py:62
  9.7 272.1 %all-gather.9.cloned.1.call-start = ((), (), s32[]{:S(2)}) async-start(), calls=%async_computation.5 | async-start | bytes 8650752 | tf_op jit(solution)/shard_map/all_gather | solution.py:62
  149.9 3.2 copy-start.1
  186.6 262.4 %all-gather.11.cloned.1.call-start = ((), (), s32[]{:S(2)}) async-start(), calls=%async_computation.6 | async-start | bytes 8650752 | tf_op jit(solution)/shard_map/all_gather | solution.py:62
  316.9 3.2 copy-start.2
  491.1 29.0 %all-to-all-start.2 = ((f32[4,1,256,512]{3,2,1,0:T(8,128)}), f32[4,1,256,512]{3,2,1,0:T(8,128)S(1)}, u32[]{:S(2)}, u32[]{:S(2)}) async-start(f32[4,1,256,512]{3,2,1,0:T(8,128)} %copy.41), calls=%async_computation.2 | async-start | bytes 4194304 | tf_op jit(solution)/shard_map/all_to_all | solution.py:15
  497.4 29.7 %copy-start.3 = (f32[1,1,256,512]{3,2,1,0:T(8,128)S(1)}, f32[1,1,256,512]{3,2,1,0:T(8,128)}, u32[]{:S(2)}) copy-start(f32[1,1,256,512]{3,2,1,0:T(8,128)} %param.12) | copy-start | bytes 1572868
Sparse Core Ops, SparseCore 0:
  11.2 101.6 all-gather.6
  186.7 95.0 all-gather.8
  353.8 95.0 all-gather.10
where the time goes:
time: 537 us; the launch traced here: 536 us
  waiting for transfers between devices  311 us (58%)
  matrix products  68.1 us (13%)
  local copies, waits for them, and re-layouts  64 us (12%)
  blocking collectives  63.5 us (12%)
  between operations  13.9 us (3%)
  other arithmetic  10.6 us (2%)
    all_gather x3, waiting for transfers between devices, on_device(): everyone = lax.all_gather(rounded, 'col', axis=0, tiled=True)  289 us
    all_to_all x2, blocking collectives, sum_at_owner(): pieces = lax.all_to_all(split_up(shard, dim, peers), axis, 0, 0, tiled=True)  57 us
    dot_general x3, matrix products, spread_terms(): jnp.einsum('tk,tiw->kiw', selector, products, precision=lax.Precision.HIG...  36.4 us
    dot_general x3, local copies, waits for them, and re-layouts, spread_terms(): jnp.einsum('tij,tjw->tiw', blocks, fetched, preferred_element_type=jnp.fl...  31.4 us
    dot_general x3, matrix products, spread_terms(): jnp.einsum('tij,tjw->tiw', blocks, fetched, preferred_element_type=jnp.fl...  22.8 us
    all_to_all x1, waiting for transfers between devices, sum_at_owner(): pieces = lax.all_to_all(split_up(shard, dim, peers), axis, 0, 0, tiled=True)  22.7 us
    gather x3, local copies, waits for them, and re-layouts, spread_terms(): fetched = jnp.take(gathered, sources, axis=0)  18.4 us
  transfers between devices with their start and end apart: 4, of which 4 were waited for; matrix products, arithmetic and copies ran while one was open for 1% of the time, Pallas kernels for 0%

commit v1 on v0

--- a/solution.py
+++ b/solution.py
@@ -59,7 +59,9 @@
         )
         solved.append(current)
         rounded = current.astype(jnp.bfloat16)[None]
-        everyone = lax.all_gather(rounded, "col", axis=0, tiled=True)
+        everyone = jnp.concatenate(
+            lax.all_to_all(jnp.stack([rounded] * lax.axis_size("col")), "col", 0, 0), axis=0
+        )
         pending = spread_terms(
             pending,
             everyone,

time: 537 us -> 831 us (1.55)
  waiting for transfers between devices: 311 us -> 566 us
  starting transfers between devices: 4.31 us -> 47 us
  between operations: 13.9 us -> 0.88 us
  local copies, waits for them, and re-layouts: 64 us -> 75 us
    all_to_all x0 -> x3, waiting for transfers between devices: none -> 546 us  [on_device(): lax.all_to_all(jnp.stack([rounded] * lax.axis_size('col')), 'col', 0, 0)]
    all_gather x3 -> x0, waiting for transfers between devices: 289 us -> none  [on_device(): everyone = lax.all_gather(rounded, 'col', axis=0, tiled=True)]
    all_to_all x0 -> x3, starting transfers between devices: none -> 43.4 us  [on_device(): lax.all_to_all(jnp.stack([rounded] * lax.axis_size('col')), 'col', 0, 0)]
    another operation x0 -> x3, local copies, waits for them, and re-layouts: none -> 12.5 us  [on_device(): jnp.stack([rounded] * lax.axis_size('col'))]
where the time goes in v1:
time: 831 us; the launch traced here: 827 us
  waiting for transfers between devices  566 us (68%)
  local copies, waits for them, and re-layouts  75 us (9%)
  matrix products  66.7 us (8%)
  blocking collectives  61.8 us (7%)
  starting transfers between devices  47 us (6%)
  other arithmetic  9.88 us (1%)
    all_to_all x3, waiting for transfers between devices, on_device(): lax.all_to_all(jnp.stack([rounded] * lax.axis_size('col')), 'col', 0, 0)  546 us
    all_to_all x2, blocking collectives, sum_at_owner(): pieces = lax.all_to_all(split_up(shard, dim, peers), axis, 0, 0, tiled=True)  53 us
    all_to_all x3, starting transfers between devices, on_device(): lax.all_to_all(jnp.stack([rounded] * lax.axis_size('col')), 'col', 0, 0)  43.4 us
    dot_general x3, matrix products, spread_terms(): jnp.einsum('tk,tiw->kiw', selector, products, precision=lax.Precision.HIG...  36.4 us
    dot_general x3, local copies, waits for them, and re-layouts, spread_terms(): jnp.einsum('tij,tjw->tiw', blocks, fetched, preferred_element_type=jnp.fl...  31.4 us
    dot_general x3, matrix products, spread_terms(): jnp.einsum('tij,tjw->tiw', blocks, fetched, preferred_element_type=jnp.fl...  22.8 us
    all_to_all x1, waiting for transfers between devices, sum_at_owner(): pieces = lax.all_to_all(split_up(shard, dim, peers), axis, 0, 0, tiled=True)  20.4 us
    gather x3, local copies, waits for them, and re-layouts, spread_terms(): fetched = jnp.take(gathered, sources, axis=0)  18.4 us
  transfers between devices with their start and end apart: 4, of which 4 were waited for; matrix products, arithmetic and copies ran while one was open for 1% of the time, Pallas kernels for 0%

profile of v1, /device:TPU:1, one launch (start us, length us, event | category | flops | bytes accessed | tf_op | source)
XLA Modules:
  0.0 827.3 jit_solution(10006433004342860348)
XLA Ops:
  2.4 4.2 stack.22
  6.6 12.1 %all-to-all-start = ((bf16[32,1,256,512]{3,2,1,0:T(8,128)(2,1)}), bf16[32,1,256,512]{3,2,1,0:T(8,128)(2,1)}, u32[]{:S(2)}, u32[]{:S(2)}) async-start(bf16[32,1,256,512]{3,2,1,0:T(8,128)(2,1)} %stack.22), calls=%async_computation | async-start | bytes 16777216 | tf_op jit(solution)/shard_map/all_to_all | solution.py:63
  20.1 186.2 %all-to-all-done = bf16[32,1,256,512]{3,2,1,0:T(8,128)(2,1)} async-done(((bf16[32,1,256,512]{3,2,1,0:T(8,128)(2,1)}), bf16[32,1,256,512]{3,2,1,0:T(8,128)(2,1)}, u32[]{:S(2)}, u32[]{:S(2)}) %all-to-all-start) | async-done | bytes 8388640 | tf_op jit(solution)/shard_map/all_to_all | solution.py:63
  206.3 6.2 gather_fusion
  212.5 7.6 fusion.9
  220.1 10.5 %copy.45 = f32[16,256,512]{2,0,1:T(8,128)} copy(f32[16,256,512]{1,2,0:T(8,128)} %fusion.9) | data formatting | bytes 16777216 | tf_op jit(solution)/shard_map/tij,tjw->tiw/dot_general | solution.py:31
  230.5 12.8 %fusion.47 = f32[12,256,512]{2,0,1:T(8,128)S(1)} fusion(f32[16,256,512]{2,0,1:T(8,128)} %copy.45, s32[16]{0:T(128)S(1)} %get-tuple-element.20, pred[16]{0:T(512)(128)(4,1)S(1)} %iota_compare_fusion.5), kind=kOutput, calls=%fused_computation.58 | convolution fusion | flops 301990272 | bytes 14680144 | tf_op jit(solution)/shard_map/tk,tiw->kiw/dot_general | solution.py:35
  247.7 28.0 %all_to_all.35 = f32[4,1,256,512]{3,2,1,0:T(8,128)S(1)} all-to-all(f32[4,1,256,512]{3,2,1,0:T(8,128)S(1)} %copy.46), channel_id=1, replica_groups=mesh['grp'=2,'row'=4,'col'=32] {'row'}, dimensions={0} | all-to-all | bytes 4194304 | tf_op jit(solution)/shard_map/all_to_all | solution.py:15
  278.7 4.2 stack.24
  282.9 16.8 %all-to-all-start.2 = ((bf16[32,1,256,512]{3,2,1,0:T(8,128)(2,1)}), bf16[32,1,256,512]{3,2,1,0:T(8,128)(2,1)}, u32[]{:S(2)}, u32[]{:S(2)}) async-start(bf16[32,1,256,512]{3,2,1,0:T(8,128)(2,1)} %stack.24), calls=%async_computation.2 | async-start | bytes 16777216 | tf_op jit(solution)/shard_map/all_to_all | solution.py:63
  300.3 179.8 %all-to-all-done.2 = bf16[32,1,256,512]{3,2,1,0:T(8,128)(2,1)} async-done(((bf16[32,1,256,512]{3,2,1,0:T(8,128)(2,1)}), bf16[32,1,256,512]{3,2,1,0:T(8,128)(2,1)}, u32[]{:S(2)}, u32[]{:S(2)}) %all-to-all-start.2) | async-done | bytes 8388640 | tf_op jit(solution)/shard_map/all_to_all | solution.py:63
  480.1 6.1 gather_fusion.1
  486.3 7.6 fusion.12
  493.9 10.5 %copy.49 = f32[16,256,512]{2,0,1:T(8,128)} copy(f32[16,256,512]{1,2,0:T(8,128)} %fusion.12) | data formatting | bytes 16777216 | tf_op jit(solution)/shard_map/tij,tjw->tiw/dot_general | solution.py:31
  504.3 10.9 %convolution_add_fusion = f32[12,256,512]{2,0,1:T(8,128)S(1)} fusion(f32[12,256,512]{2,0,1:T(8,128)} %copy-done.1, f32[16,256,512]{2,0,1:T(8,128)} %copy.49, s32[16]{0:T(128)S(1)} %get-tuple-element.21, pred[16]{0:T(512)(128)(4,1)S(1)} %iota_compare_fusion.4), kind=kOutput, calls=%fused_computation.12 | convolution fusion | flops 303563136 | bytes 20971600 | tf_op jit(solution)/shard_map/tk,tiw->kiw/dot_general | solution.py:35
  519.7 25.1 %all_to_all.36 = f32[4,1,256,512]{3,2,1,0:T(8,128)S(1)} all-to-all(f32[4,1,256,512]{3,2,1,0:T(8,128)S(1)} %copy.50), channel_id=1, replica_groups=mesh['grp'=2,'row'=4,'col'=32] {'row'}, dimensions={0} | all-to-all | bytes 4194304 | tf_op jit(solution)/shard_map/all_to_all | solution.py:15
  552.7 14.4 %all-to-all-start.4 = ((bf16[32,1,256,512]{3,2,1,0:T(8,128)(2,1)}), bf16[32,1,256,512]{3,2,1,0:T(8,128)(2,1)}, u32[]{:S(2)}, u32[]{:S(2)}) async-start(bf16[32,1,256,512]{3,2,1,0:T(8,128)(2,1)} %stack.27), calls=%async_computation.4 | async-start | bytes 16777216 | tf_op jit(solution)/shard_map/all_to_all | solution.py:63
  567.8 179.7 %all-to-all-done.4 = bf16[32,1,256,512]{3,2,1,0:T(8,128)(2,1)} async-done(((bf16[32,1,256,512]{3,2,1,0:T(8,128)(2,1)}), bf16[32,1,256,512]{3,2,1,0:T(8,128)(2,1)}, u32[]{:S(2)}, u32[]{:S(2)}) %all-to-all-start.4) | async-done | bytes 8388640 | tf_op jit(solution)/shard_map/all_to_all | solution.py:63
  747.6 6.1 gather_fusion.2
  753.7 7.6 fusion.15
  761.3 10.5 %copy.53 = f32[16,256,512]{2,0,1:T(8,128)} copy(f32[16,256,512]{1,2,0:T(8,128)} %fusion.15) | data formatting | bytes 16777216 | tf_op jit(solution)/shard_map/tij,tjw->tiw/dot_general | solution.py:31
  771.8 12.8 %fusion.54 = f32[12,256,512]{2,0,1:T(8,128)S(1)} fusion(f32[16,256,512]{2,0,1:T(8,128)} %copy.53, s32[16]{0:T(128)S(1)} %get-tuple-element.19, pred[16]{0:T(512)(128)(4,1)S(1)} %iota_compare_fusion.3), kind=kOutput, calls=%fused_computation.63 | convolution fusion | flops 301990272 | bytes 14680144 | tf_op jit(solution)/shard_map/tk,tiw->kiw/dot_general | solution.py:35
  795.7 20.4 %all-to-all-done.5 = f32[4,1,256,512]{3,2,1,0:T(8,128)S(1)} async-done(((f32[4,1,256,512]{3,2,1,0:T(8,128)}), f32[4,1,256,512]{3,2,1,0:T(8,128)S(1)}, u32[]{:S(2)}, u32[]{:S(2)}) %all-to-all-start.5) | async-done | bytes 2097184 | tf_op jit(solution)/shard_map/all_to_all | solution.py:15
  816.4 8.7 %all_to_all.37 = f32[2,256,512]{2,1,0:T(8,128)S(1)} all-to-all(f32[2,256,512]{2,1,0:T(8,128)S(1)} %broadcast_in_dim.25), channel_id=1, replica_groups=mesh['grp'=2,'row'=4,'col'=32] {'grp'}, dimensions={0} | all-to-all | bytes 2097152 | tf_op jit(solution)/shard_map/all_to_all | solution.py:21
  (42 shorter events, 37.8 us)
Async XLA Ops:
  0.6 824.7 %copy-start = (f32[1,1,256,256]{3,2,1,0:T(8,128)S(1)}, f32[1,1,256,256]{3,2,1,0:T(8,128)}, u32[]{:S(2)}) copy-start(f32[1,1,256,256]{3,2,1,0:T(8,128)} %param.13) | copy-start | bytes 786436
  6.6 12.1 %copy-start.4 = (s32[1,1,1,3]{3,2,1,0:T(1,128)S(1)}, s32[1,1,1,3]{3,2,1,0:T(1,128)}, u32[]{:S(2)}) copy-start(s32[1,1,1,3]{3,2,1,0:T(1,128)} %param.17) | copy-start | bytes 40
  6.6 13.4 %copy-start.6 = (s32[1,1,1,3,16]{4,2,3,1,0:T(1,128)S(1)}, s32[1,1,1,3,16]{4,2,3,1,0:T(1,128)}, u32[]{:S(2)}) copy-start(s32[1,1,1,3,16]{4,2,3,1,0:T(1,128)} %param.16) | copy-start | bytes 580
  6.6 13.5 %copy-start.5 = (s32[1,1,1,3,16]{4,2,3,1,0:T(1,128)S(1)}, s32[1,1,1,3,16]{4,2,3,1,0:T(1,128)}, u32[]{:S(2)}) copy-start(s32[1,1,1,3,16]{4,2,3,1,0:T(1,128)} %param.15) | copy-start | bytes 580
  6.6 199.7 %all-to-all-start = ((bf16[32,1,256,512]{3,2,1,0:T(8,128)(2,1)}), bf16[32,1,256,512]{3,2,1,0:T(8,128)(2,1)}, u32[]{:S(2)}, u32[]{:S(2)}) async-start(bf16[32,1,256,512]{3,2,1,0:T(8,128)(2,1)} %stack.22), calls=%async_computation | async-start | bytes 16777216 | tf_op jit(solution)/shard_map/all_to_all | solution.py:63
  243.3 3.2 copy-start.1
  282.9 197.3 %all-to-all-start.2 = ((bf16[32,1,256,512]{3,2,1,0:T(8,128)(2,1)}), bf16[32,1,256,512]{3,2,1,0:T(8,128)(2,1)}, u32[]{:S(2)}, u32[]{:S(2)}) async-start(bf16[32,1,256,512]{3,2,1,0:T(8,128)(2,1)} %stack.24), calls=%async_computation.2 | async-start | bytes 16777216 | tf_op jit(solution)/shard_map/all_to_all | solution.py:63
  515.2 3.2 copy-start.2
  552.7 194.9 %all-to-all-start.4 = ((bf16[32,1,256,512]{3,2,1,0:T(8,128)(2,1)}), bf16[32,1,256,512]{3,2,1,0:T(8,128)(2,1)}, u32[]{:S(2)}, u32[]{:S(2)}) async-start(bf16[32,1,256,512]{3,2,1,0:T(8,128)(2,1)} %stack.27), calls=%async_computation.4 | async-start | bytes 16777216 | tf_op jit(solution)/shard_map/all_to_all | solution.py:63
  789.7 26.3 %all-to-all-start.5 = ((f32[4,1,256,512]{3,2,1,0:T(8,128)}), f32[4,1,256,512]{3,2,1,0:T(8,128)S(1)}, u32[]{:S(2)}, u32[]{:S(2)}) async-start(f32[4,1,256,512]{3,2,1,0:T(8,128)} %copy.54), calls=%async_computation.5 | async-start | bytes 4194304 | tf_op jit(solution)/shard_map/all_to_all | solution.py:15
  795.7 29.6 %copy-start.3 = (f32[1,1,256,512]{3,2,1,0:T(8,128)S(1)}, f32[1,1,256,512]{3,2,1,0:T(8,128)}, u32[]{:S(2)}) copy-start(f32[1,1,256,512]{3,2,1,0:T(8,128)} %param.12) | copy-start | bytes 1572868
